TPU v7x, 32 devices: a whole 2x2x4 slice. The times are simulated.
32 devices in a mesh: pts: 8 (over y, x, core), val: 4 (over z).
Axes of the slice: x: 2, y: 2, z: 4, core: 2. Of those that a mesh axis runs over, the one named last changes fastest.
Arguments:
- vectors: float32 [1, 512, 2048], P(None, 'val', 'pts'), may hold values from -6 to 6
- eval_energy: float32 [512], P('val'), may hold values from -2 to -0.2
- cond_energy: float32 [2048], P('pts'), may hold values from 0.2 to 2
- val_orbitals: float32 [512, 8192], P('pts', 'val'), may hold values from -0.25 to 0.25
- cond_orbitals: float32 [2048, 8192], P('val', 'pts'), may hold values from -0.125 to 0.125
- screened: float32 [8192, 8192], P('val', 'pts'), may hold values from -1.5 to 1.5
Outputs:
- filtered: float32 [1, 512, 2048], P(None, 'val', 'pts')
All inputs are finite; a program needn't handle non-finite values.
Results may differ from a plain program's by a relative error of at most 0.00013.
Values sent between devices are 32-bit elements; how exact they have to be, the bound alone decides.
A program may use at most 128 MiB of HBM per device.

v0:
```python
import jax
import jax.numpy as jnp
from jax import lax
from jax.sharding import PartitionSpec as P

ITERS = 2
CENTER = 2.2
HALF_WIDTH = 2.0


def per_device(vectors, eval_energy, cond_energy, val_orbitals, cond_orbitals, screened):
    highest = lax.Precision.HIGHEST
    cond_whole = lax.all_gather(cond_orbitals, "val", axis=0, tiled=True)
    val_whole = lax.all_gather(val_orbitals, "pts", axis=0, tiled=True)
    ediff = cond_energy[None, None, :] - eval_energy[None, :, None]
    older = vectors
    newer = vectors
    for step in range(ITERS):
        direct_full_x = lax.all_gather(newer, "pts", axis=2, tiled=True)
        pair = jnp.einsum(
            "bvc,cn->bvn",
            direct_full_x,
            cond_whole,
            precision=highest,
            preferred_element_type=jnp.float32,
        )
        pair_all = lax.all_gather(pair, "val", axis=1, tiled=True)
        mixed = jnp.einsum(
            "vm,bvn->bmn",
            val_whole,
            pair_all,
            precision=highest,
            preferred_element_type=jnp.float32,
        )
        weighted = mixed * screened[None, :, :]
        back_terms = jnp.einsum(
            "vm,bmn->bvn",
            val_whole,
            weighted,
            precision=highest,
            preferred_element_type=jnp.float32,
        )
        back = lax.psum_scatter(back_terms, "val", scatter_dimension=1, tiled=True)
        hamil = ediff * newer - lax.psum_scatter(
            jnp.einsum(
                "bvn,cn->bvc",
                back,
                cond_whole,
                precision=highest,
                preferred_element_type=jnp.float32,
            ),
            "pts",
            scatter_dimension=2,
            tiled=True,
        )
        scaled = (hamil - CENTER * newer) / HALF_WIDTH
        if step == 0:
            following = scaled
        else:
            following = 2.0 * scaled - older
        older = newer
        newer = following
    return newer


def solution(mesh):
    placed = (
        P(None, "val", "pts"),
        P("val"),
        P("pts"),
        P("pts", "val"),
        P("val", "pts"),
        P("val", "pts"),
    )
    return jax.shard_map(
        per_device, mesh=mesh, in_specs=placed, out_specs=P(None, "val", "pts"), check_vma=False
    )
```

profile of v0, /device:TPU:0, one launch (start us, length us, event | category | flops | bytes accessed | tf_op | source)
XLA Modules:
  0.0 608.8 jit_solution(13954029730441035257)
XLA Ops:
  6.5 0.0 all-gather.9.cloned.1.call-start
  6.5 0.7 all-gather.9.cloned.1.call-update
  7.3 0.0 all-gather.11.cloned.1.call-start
  7.3 0.7 all-gather.11.cloned.1.call-update
  8.0 0.0 all-gather.13.cloned.1.call-start
  8.1 0.7 all-gather.13.cloned.1.call-update
  8.7 0.0 all-gather.17.cloned.1.call-start
  8.8 26.7 %all-gather.9.cloned.1.call-done = f32[1,128,2048]{2,1,0:T(8,128)} async-done(((f32[1,128,256]{2,1,0:T(8,128)}), f32[1,128,2048]{2,1,0:T(8,128)}) %all-gather.9.cloned.1.call-update) | async-done | bytes 1048592 | tf_op jit(solution)/shard_map/all_gather | solution.py:19
  35.4 151.2 %all-gather.11.cloned.1.call-done = f32[2048,1024]{1,0:T(8,128)} async-done(((f32[512,1024]{1,0:T(8,128)}), f32[2048,1024]{1,0:T(8,128)}) %all-gather.11.cloned.1.call-update) | async-done | bytes 8388624 | tf_op jit(solution)/shard_map/all_gather | solution.py:13
  186.7 9.2 %fusion.16 = f32[128,1024]{1,0:T(8,128)} fusion(f32[2048,1024]{1,0:T(8,128)} %all-gather.11.cloned.1.call-done, f32[1,128,2048]{2,1,0:T(8,128)} %all-gather.9.cloned.1.call-done), kind=kOutput, calls=%fused_computation.14 | convolution fusion | flops 3221225472 | bytes 9961472 | tf_op jit(solution)/shard_map/bvc,cn->bvn/dot_general | solution.py:20
  195.8 0.0 all-gather.17.cloned.1.call-update
  195.8 0.2 reduce-scatter.5.cloned.1.call-start
  196.1 9.1 %copy.7 = f32[2048,1024]{0,1:T(8,128)} copy(f32[2048,1024]{1,0:T(8,128)} %param.11) | data formatting | bytes 16777216 | tf_op args[5]
  205.2 18.1 %all-gather.13.cloned.1.call-done = f32[512,2048]{1,0:T(8,128)} async-done(((f32[64,2048]{1,0:T(8,128)}), f32[512,2048]{1,0:T(8,128)}) %all-gather.13.cloned.1.call-update) | async-done | bytes 4194320 | tf_op jit(solution)/shard_map/all_gather | solution.py:14
  223.3 47.1 %all-gather.17.cloned.1.call-done = f32[512,1024]{1,0:T(8,128)} async-done(((f32[128,1024]{1,0:T(8,128)}), f32[512,1024]{1,0:T(8,128)}) %all-gather.17.cloned.1.call-update) | async-done | bytes 2097168 | tf_op jit(solution)/shard_map/all_gather | solution.py:27
  270.5 0.0 copy-start
  270.5 0.0 copy-start.1
  270.5 17.0 %fusion.26 = f32[1024,2048]{1,0:T(8,128)S(1)} fusion(f32[512,1024]{1,0:T(8,128)} %all-gather.17.cloned.1.call-done, f32[512,2048]{1,0:T(8,128)} %all-gather.13.cloned.1.call-done), kind=kOutput, calls=%fused_computation.26 | convolution fusion | flops 12884901888 | bytes 14680064 | tf_op jit(solution)/shard_map/vm,bvn->bmn/dot_general | solution.py:28
  287.4 0.0 copy-done
  287.4 0.0 copy-done.1
  287.5 15.3 %fusion.8 = f32[1,512,1024]{1,2,0:T(8,128)} fusion(f32[512,2048]{1,0:T(8,128)S(1)} %copy-done.1, f32[1024,2048]{1,0:T(8,128)S(1)} %fusion.26, f32[2048,1024]{0,1:T(8,128)S(1)} %copy-done), kind=kOutput, calls=%fused_computation.10 | convolution fusion | flops 12886999040 | bytes 23068672 | tf_op jit(solution)/shard_map/vm,bmn->bvn/dot_general | solution.py:36
  302.8 0.0 copy-start.3
  302.8 0.0 copy-start.5
  302.8 0.0 copy-start.6
  302.8 0.0 reduce-scatter.5.cloned.1.call-update
  302.8 0.3 reduce-scatter.7.cloned.1.call-start
  303.1 42.3 %reduce-scatter.5.cloned.1.call-done = f32[1,128,1024]{1,2,0:T(8,128)} async-done(((f32[1,512,1024]{1,2,0:T(8,128)}), f32[1,128,1024]{1,2,0:T(8,128)}) %reduce-scatter.5.cloned.1.call-update) | async-done | bytes 524304 | tf_op jit(solution)/shard_map/reduce_scatter | solution.py:43
  345.4 13.4 %convolution_bitcast_fusion.1 = f32[1,128,2048]{2,1,0:T(8,128)} fusion(f32[2048,1024]{1,0:T(8,128)} %all-gather.11.cloned.1.call-done, f32[1,128,1024]{1,2,0:T(8,128)} %reduce-scatter.5.cloned.1.call-done), kind=kOutput, calls=%fused_computation.9 | convolution fusion | flops 3221225472 | bytes 9961472 | tf_op jit(solution)/shard_map/bvn,cn->bvc/dot_general | solution.py:45
  358.8 0.0 reduce-scatter.7.cloned.1.call-update
  358.8 0.0 all-gather.15.cloned.1.call-start
  358.8 35.3 %reduce-scatter.7.cloned.1.call-done = f32[1,128,256]{2,1,0:T(8,128)} async-done(((f32[1,128,2048]{2,1,0:T(8,128)}), f32[1,128,256]{2,1,0:T(8,128)}) %reduce-scatter.7.cloned.1.call-update) | async-done | bytes 131088 | tf_op jit(solution)/shard_map/reduce_scatter | solution.py:44
  394.1 0.0 copy-done.3
  394.1 0.0 copy-done.5
  394.1 0.0 copy-done.6
  394.1 1.7 fusion.25
  395.8 0.0 all-gather.15.cloned.1.call-update
  395.8 0.0 all-gather.19.cloned.1.call-start
  395.8 23.6 %all-gather.15.cloned.1.call-done = f32[1,128,2048]{2,1,0:T(8,128)} async-done(((f32[1,128,256]{2,1,0:T(8,128)}), f32[1,128,2048]{2,1,0:T(8,128)}) %all-gather.15.cloned.1.call-update) | async-done | bytes 1048592 | tf_op jit(solution)/shard_map/all_gather | solution.py:19
  419.5 9.2 %fusion.14 = f32[128,1024]{1,0:T(8,128)} fusion(f32[2048,1024]{1,0:T(8,128)} %all-gather.11.cloned.1.call-done, f32[1,128,2048]{2,1,0:T(8,128)} %all-gather.15.cloned.1.call-done), kind=kOutput, calls=%fused_computation.12 | convolution fusion | flops 3221225472 | bytes 9961472 | tf_op jit(solution)/shard_map/bvc,cn->bvn/dot_general | solution.py:20
  428.6 0.0 all-gather.19.cloned.1.call-update
  428.7 0.4 reduce-scatter.9.cloned.1.call-start
  429.1 45.4 %all-gather.19.cloned.1.call-done = f32[512,1024]{1,0:T(8,128)} async-done(((f32[128,1024]{1,0:T(8,128)}), f32[512,1024]{1,0:T(8,128)}) %all-gather.19.cloned.1.call-update) | async-done | bytes 2097168 | tf_op jit(solution)/shard_map/all_gather | solution.py:27
  474.5 0.0 copy-start.2
  474.5 16.9 %fusion.27 = f32[1024,2048]{1,0:T(8,128)S(1)} fusion(f32[512,1024]{1,0:T(8,128)} %all-gather.19.cloned.1.call-done, f32[512,2048]{1,0:T(8,128)} %all-gather.13.cloned.1.call-done), kind=kOutput, calls=%fused_computation.27 | convolution fusion | flops 12884901888 | bytes 14680064 | tf_op jit(solution)/shard_map/vm,bvn->bmn/dot_general | solution.py:28
  491.4 0.0 copy-done.2
  491.4 17.3 %fusion.11 = f32[1,512,1024]{1,2,0:T(8,128)} fusion(f32[512,2048]{1,0:T(8,128)S(1)} %copy-done.2, f32[1024,2048]{1,0:T(8,128)S(1)} %fusion.27, f32[2048,1024]{0,1:T(8,128)} %copy.7), kind=kOutput, calls=%fused_computation.11 | convolution fusion | flops 12886999040 | bytes 23068672 | tf_op jit(solution)/shard_map/vm,bmn->bvn/dot_general | solution.py:36
  508.7 0.0 copy-start.4
  508.7 0.0 reduce-scatter.9.cloned.1.call-update
  508.7 0.2 reduce-scatter.11.cloned.1.call-start
  508.9 42.4 %reduce-scatter.9.cloned.1.call-done = f32[1,128,1024]{1,2,0:T(8,128)} async-done(((f32[1,512,1024]{1,2,0:T(8,128)}), f32[1,128,1024]{1,2,0:T(8,128)}) %reduce-scatter.9.cloned.1.call-update) | async-done | bytes 524304 | tf_op jit(solution)/shard_map/reduce_scatter | solution.py:43
  551.3 13.4 %convolution_bitcast_fusion = f32[1,128,2048]{2,1,0:T(8,128)} fusion(f32[2048,1024]{1,0:T(8,128)} %all-gather.11.cloned.1.call-done, f32[1,128,1024]{1,2,0:T(8,128)} %reduce-scatter.9.cloned.1.call-done), kind=kOutput, calls=%fused_computation.8 | convolution fusion | flops 3221225472 | bytes 9961472 | tf_op jit(solution)/shard_map/bvn,cn->bvc/dot_general | solution.py:45
  564.8 0.0 reduce-scatter.11.cloned.1.call-update
  564.8 35.3 %reduce-scatter.11.cloned.1.call-done = f32[1,128,256]{2,1,0:T(8,128)} async-done(((f32[1,128,2048]{2,1,0:T(8,128)}), f32[1,128,256]{2,1,0:T(8,128)}) %reduce-scatter.11.cloned.1.call-update) | async-done | bytes 131088 | tf_op jit(solution)/shard_map/reduce_scatter | solution.py:44
  600.1 0.0 copy-done.4
  600.1 1.7 fusion.24
Async XLA Ops:
  6.5 28.9 %all-gather.9.cloned.1.call-start = ((), (), s32[]{:S(2)}) async-start(), calls=%async_computation.4 | async-start | bytes 1179648 | tf_op jit(solution)/shard_map/all_gather | solution.py:19
  7.3 179.4 %all-gather.11.cloned.1.call-start = ((), (), s32[]{:S(2)}) async-start(), calls=%async_computation.5 | async-start | bytes 10485760 | tf_op jit(solution)/shard_map/all_gather | solution.py:13
  8.0 215.3 %all-gather.13.cloned.1.call-start = ((), (), s32[]{:S(2)}) async-start(), calls=%async_computation.6 | async-start | bytes 4718592 | tf_op jit(solution)/shard_map/all_gather | solution.py:14
  8.7 261.7 %all-gather.17.cloned.1.call-start = ((), (), s32[]{:S(2)}) async-start(), calls=%async_computation.12 | async-start | bytes 2621440 | tf_op jit(solution)/shard_map/all_gather | solution.py:27
  195.8 149.5 %reduce-scatter.5.cloned.1.call-start = ((), (), s32[]{:S(2)}) async-start(), calls=%async_computation.7 | async-start | bytes 2621440 | tf_op jit(solution)/shard_map/reduce_scatter | solution.py:43
  270.5 17.0 %copy-start = (f32[2048,1024]{0,1:T(8,128)S(1)}, f32[2048,1024]{0,1:T(8,128)}, u32[]{:S(2)}) copy-start(f32[2048,1024]{0,1:T(8,128)} %copy.7) | copy-start | bytes 25165828
  270.5 17.0 %copy-start.1 = (f32[512,2048]{1,0:T(8,128)S(1)}, f32[512,2048]{1,0:T(8,128)}, u32[]{:S(2)}) copy-start(f32[512,2048]{1,0:T(8,128)} %all-gather.13.cloned.1.call-done) | copy-start | bytes 12582916
  302.8 91.3 %copy-start.3 = (f32[1,128,256]{2,1,0:T(8,128)S(1)}, f32[1,128,256]{2,1,0:T(8,128)}, u32[]{:S(2)}) copy-start(f32[1,128,256]{2,1,0:T(8,128)} %param.6) | copy-start | bytes 393220
  302.8 91.3 %copy-start.5 = (f32[256]{0:T(256)S(1)}, f32[256]{0:T(256)}, u32[]{:S(2)}) copy-start(f32[256]{0:T(256)} %param.8) | copy-start | bytes 3076
  302.8 91.3 %copy-start.6 = (f32[128]{0:T(128)S(1)}, f32[128]{0:T(128)}, u32[]{:S(2)}) copy-start(f32[128]{0:T(128)} %param.7) | copy-start | bytes 1540
  302.8 91.3 %reduce-scatter.7.cloned.1.call-start = ((), (), s32[]{:S(2)}) async-start(), calls=%async_computation.8 | async-start | bytes 1179648 | tf_op jit(solution)/shard_map/reduce_scatter | solution.py:44
  358.8 60.7 %all-gather.15.cloned.1.call-start = ((), (), s32[]{:S(2)}) async-start(), calls=%async_computation.9 | async-start | bytes 1179648 | tf_op jit(solution)/shard_map/all_gather | solution.py:19
  395.8 78.7 %all-gather.19.cloned.1.call-start = ((), (), s32[]{:S(2)}) async-start(), calls=%async_computation.13 | async-start | bytes 2621440 | tf_op jit(solution)/shard_map/all_gather | solution.py:27
  428.7 122.7 %reduce-scatter.9.cloned.1.call-start = ((), (), s32[]{:S(2)}) async-start(), calls=%async_computation.10 | async-start | bytes 2621440 | tf_op jit(solution)/shard_map/reduce_scatter | solution.py:43
  474.5 17.0 %copy-start.2 = (f32[512,2048]{1,0:T(8,128)S(1)}, f32[512,2048]{1,0:T(8,128)}, u32[]{:S(2)}) copy-start(f32[512,2048]{1,0:T(8,128)} %all-gather.13.cloned.1.call-done) | copy-start | bytes 12582916
  508.7 91.4 %copy-start.4 = (f32[1,128,256]{2,1,0:T(8,128)S(1)}, f32[1,128,256]{2,1,0:T(8,128)}, u32[]{:S(2)}) copy-start(f32[1,128,256]{2,1,0:T(8,128)} %reduce-scatter.7.cloned.1.call-done) | copy-start | bytes 393220
  508.7 91.4 %reduce-scatter.11.cloned.1.call-start = ((), (), s32[]{:S(2)}) async-start(), calls=%async_computation.11 | async-start | bytes 1179648 | tf_op jit(solution)/shard_map/reduce_scatter | solution.py:44
Sparse Core Ops, SparseCore 0:
  9.2 26.1 all-gather.8
  37.0 149.5 all-gather.10
  188.5 34.7 all-gather.12
  224.8 45.6 all-gather.16
  302.9 42.4 reduce-scatter.4
  358.9 35.1 reduce-scatter.6
  396.0 23.4 all-gather.14
  428.8 45.6 all-gather.18
  508.8 42.4 reduce-scatter.8
  564.9 35.1 reduce-scatter.10
where the time goes:
time: 613 us; the launch traced here: 609 us
  waiting for transfers between devices  470 us (77%)
  matrix products  112 us (18%)
  between operations  13.8 us (2%)
  local copies, waits for them, and re-layouts  9.17 us (1%)
    all_gather x1, waiting for transfers between devices, per_device(): cond_whole = lax.all_gather(cond_orbitals, 'val', axis=0, tiled=True)  151 us
    all_gather x2, waiting for transfers between devices, per_device(): pair_all = lax.all_gather(pair, 'val', axis=1, tiled=True)  92.5 us
    reduce_scatter x2, waiting for transfers between devices, per_device(): back = lax.psum_scatter(back_terms, 'val', scatter_dimension=1, tiled=True)  84.7 us
    reduce_scatter x2, waiting for transfers between devices, per_device(): lax.psum_scatter(jnp.einsum('bvn,cn->bvc', back, cond_whole, precision=hi...  70.5 us
    all_gather x2, waiting for transfers between devices, per_device(): direct_full_x = lax.all_gather(newer, 'pts', axis=2, tiled=True)  50.3 us
    dot_general x2, matrix products, per_device(): jnp.einsum('vm,bvn->bmn', val_whole, pair_all, precision=highest, preferr...  33.9 us
    dot_general x2, matrix products, per_device(): jnp.einsum('vm,bmn->bvn', val_whole, weighted, precision=highest, preferr...  32.6 us
    dot_general x2, matrix products, per_device(): jnp.einsum('bvn,cn->bvc', back, cond_whole, precision=highest, preferred_...  26.8 us
  transfers between devices with their start and end apart: 10, of which 10 were waited for; matrix products, arithmetic and copies ran while one was open for 3% of the time, Pallas kernels for 0%

commit v1 on v0

--- a/solution.py
+++ b/solution.py
@@ -24,7 +24,14 @@
             precision=highest,
             preferred_element_type=jnp.float32,
         )
-        pair_all = lax.all_gather(pair, "val", axis=1, tiled=True)
+        ring = [pair]
+        for hop in range(3):
+            ring.append(lax.ppermute(ring[-1], "val", [(dev, (dev + 1) % 4) for dev in range(4)]))
+        pair_all = jnp.roll(
+            jnp.concatenate(ring[::-1], axis=1),
+            (lax.axis_index("val") + 1) * ring[0].shape[1],
+            axis=1,
+        )
         mixed = jnp.einsum(
             "vm,bvn->bmn",
             val_whole,

time: 613 us -> 577 us (0.941)
  waiting for transfers between devices: 470 us -> 435 us
    all_gather x2 -> x0, waiting for transfers between devices: 92.5 us -> none  [per_device(): pair_all = lax.all_gather(pair, 'val', axis=1, tiled=True)]
    ppermute x0 -> x6, waiting for transfers between devices: none -> 78.7 us  [per_device(): lax.ppermute(ring[-1], 'val', [(dev, (dev + 1) % 4) for dev in range(4)])]
    all_gather x1, waiting for transfers between devices: 18.1 us -> 0.01 us  [per_device(): val_whole = lax.all_gather(val_orbitals, 'pts', axis=0, tiled=True)]
  transfers between devices with their start and end apart: 10 -> 14, of which waited for: 10 -> 13; matrix products, arithmetic and copies ran while one was open for 3% -> 3% of each run, Pallas kernels for 0% -> 0%
where the time goes in v1:
time: 577 us; the launch traced here: 574 us
  waiting for transfers between devices  435 us (75%)
  matrix products  110 us (19%)
  between operations  13.9 us (2%)
  local copies, waits for them, and re-layouts  9.19 us (2%)
    all_gather x1, waiting for transfers between devices, per_device(): cond_whole = lax.all_gather(cond_orbitals, 'val', axis=0, tiled=True)  151 us
    reduce_scatter x2, waiting for transfers between devices, per_device(): back = lax.psum_scatter(back_terms, 'val', scatter_dimension=1, tiled=True)  82.5 us
    ppermute x6, waiting for transfers between devices, per_device(): lax.ppermute(ring[-1], 'val', [(dev, (dev + 1) % 4) for dev in range(4)])  78.7 us
    reduce_scatter x2, waiting for transfers between devices, per_device(): lax.psum_scatter(jnp.einsum('bvn,cn->bvc', back, cond_whole, precision=hi...  70.6 us
    all_gather x2, waiting for transfers between devices, per_device(): direct_full_x = lax.all_gather(newer, 'pts', axis=2, tiled=True)  50.2 us
    dot_general x2, matrix products, per_device(): jnp.einsum('vm,bvn->bmn', val_whole, pair_all, precision=highest, preferr...  36.9 us
    dot_general x2, matrix products, per_device(): jnp.einsum('vm,bmn->bvn', val_whole, weighted, precision=highest, preferr...  30.9 us
    dot_general x2, matrix products, per_device(): jnp.einsum('bvn,cn->bvc', back, cond_whole, precision=highest, preferred_...  26.8 us
  transfers between devices with their start and end apart: 14, of which 13 were waited for; matrix products, arithmetic and copies ran while one was open for 3% of the time, Pallas kernels for 0%

profile of v1, /device:TPU:0, one launch (start us, length us, event | category | flops | bytes accessed | tf_op | source)
XLA Modules:
  0.0 574.3 jit_solution(6192828571499579017)
XLA Ops:
  6.5 0.0 all-gather.5.cloned.1.call-start
  6.5 0.7 all-gather.5.cloned.1.call-update
  7.3 0.0 all-gather.7.cloned.1.call-start
  7.3 0.7 all-gather.7.cloned.1.call-update
  8.0 0.0 all-gather.9.cloned.1.call-start
  8.1 0.7 all-gather.9.cloned.1.call-update
  8.7 0.0 reduce-scatter.5.cloned.1.call-start
  8.8 26.7 %all-gather.5.cloned.1.call-done = f32[1,128,2048]{2,1,0:T(8,128)} async-done(((f32[1,128,256]{2,1,0:T(8,128)}), f32[1,128,2048]{2,1,0:T(8,128)}) %all-gather.5.cloned.1.call-update) | async-done | bytes 1048592 | tf_op jit(solution)/shard_map/all_gather | solution.py:19
  35.4 151.2 %all-gather.7.cloned.1.call-done = f32[2048,1024]{1,0:T(8,128)} async-done(((f32[512,1024]{1,0:T(8,128)}), f32[2048,1024]{1,0:T(8,128)}) %all-gather.7.cloned.1.call-update) | async-done | bytes 8388624 | tf_op jit(solution)/shard_map/all_gather | solution.py:13
  186.7 7.5 %convolution_bitcast_fusion.3 = f32[1,128,1024]{2,1,0:T(8,128)S(1)} fusion(f32[2048,1024]{1,0:T(8,128)} %all-gather.7.cloned.1.call-done, f32[1,128,2048]{2,1,0:T(8,128)} %all-gather.5.cloned.1.call-done), kind=kOutput, calls=%fused_computation.47 | convolution fusion | flops 3221225472 | bytes 9961472 | tf_op jit(solution)/shard_map/bvc,cn->bvn/dot_general | solution.py:20
  194.2 0.1 collective-permute-start
  194.2 15.6 %collective-permute-done = f32[1,128,1024]{2,1,0:T(8,128)S(1)} collective-permute-done((f32[1,128,1024]{2,1,0:T(8,128)S(1)}, f32[1,128,1024]{2,1,0:T(8,128)S(1)}, u32[]{:S(2)}, u32[]{:S(2)}) %collective-permute-start) | collective-permute-done | bytes 524320 | tf_op jit(solution)/shard_map/ppermute | solution.py:29
  209.8 0.0 collective-permute-start.1
  209.8 14.8 %collective-permute-done.1 = f32[1,128,1024]{2,1,0:T(8,128)S(1)} collective-permute-done((f32[1,128,1024]{2,1,0:T(8,128)S(1)}, f32[1,128,1024]{2,1,0:T(8,128)S(1)}, u32[]{:S(2)}, u32[]{:S(2)}) %collective-permute-start.1) | collective-permute-done | bytes 524320 | tf_op jit(solution)/shard_map/ppermute | solution.py:29
  224.6 0.2 collective-permute-start.2
  224.8 9.1 %copy.7 = f32[2048,1024]{0,1:T(8,128)} copy(f32[2048,1024]{1,0:T(8,128)} %param.13) | data formatting | bytes 16777216 | tf_op args[5]
  233.9 0.0 all-gather.9.cloned.1.call-done
  233.9 0.0 copy-start.1
  233.9 4.7 collective-permute-done.2
  238.7 0.0 copy-start
  238.7 20.1 %fusion.24 = f32[1024,2048]{1,0:T(8,128)S(1)} fusion(f32[512,2048]{1,0:T(8,128)} %all-gather.9.cloned.1.call-done, s32[]{:T(128)S(6)} %select_n.13, f32[1,128,1024]{2,1,0:T(8,128)S(1)} %collective-permute-done.2, f32[1,128,1024]{2,1,0:T(8,128)S(1)} %collective-permute-done.1, f32[1,128,1024]{2,1,0:T(8,128)S(1)} %collective-permute-done, ...), kind=kOutput, calls=%fused_computation.40 | convolution fusion | flops 12888571904 | bytes 14680068 | tf_op jit(solution)/shard_map/vm,bvn->bmn/dot_general | solution.py:35
  258.8 0.0 copy-done.1
  258.8 0.0 copy-done
  258.8 15.5 %fusion.30 = f32[1,512,1024]{1,2,0:T(8,128)} fusion(f32[512,2048]{1,0:T(8,128)S(1)} %copy-done.1, f32[1024,2048]{1,0:T(8,128)S(1)} %fusion.24, f32[2048,1024]{0,1:T(8,128)S(1)} %copy-done), kind=kOutput, calls=%fused_computation.44 | convolution fusion | flops 12886999040 | bytes 23068672 | tf_op jit(solution)/shard_map/vm,bmn->bvn/dot_general | solution.py:43
  274.4 0.0 reduce-scatter.5.cloned.1.call-update
  274.4 0.0 copy-start.3
  274.4 0.0 copy-start.5
  274.4 0.0 copy-start.6
  274.4 0.0 reduce-scatter.7.cloned.1.call-start
  274.5 41.8 %reduce-scatter.5.cloned.1.call-done = f32[1,128,1024]{1,2,0:T(8,128)} async-done(((f32[1,512,1024]{1,2,0:T(8,128)}), f32[1,128,1024]{1,2,0:T(8,128)}) %reduce-scatter.5.cloned.1.call-update) | async-done | bytes 524304 | tf_op jit(solution)/shard_map/reduce_scatter | solution.py:50
  316.3 13.4 %convolution_bitcast_fusion.1 = f32[1,128,2048]{2,1,0:T(8,128)} fusion(f32[2048,1024]{1,0:T(8,128)} %all-gather.7.cloned.1.call-done, f32[1,128,1024]{1,2,0:T(8,128)} %reduce-scatter.5.cloned.1.call-done), kind=kOutput, calls=%fused_computation.25 | convolution fusion | flops 3221225472 | bytes 9961472 | tf_op jit(solution)/shard_map/bvn,cn->bvc/dot_general | solution.py:52
  329.7 0.0 reduce-scatter.7.cloned.1.call-update
  329.7 0.0 all-gather.11.cloned.1.call-start
  329.7 35.3 %reduce-scatter.7.cloned.1.call-done = f32[1,128,256]{2,1,0:T(8,128)} async-done(((f32[1,128,2048]{2,1,0:T(8,128)}), f32[1,128,256]{2,1,0:T(8,128)}) %reduce-scatter.7.cloned.1.call-update) | async-done | bytes 131088 | tf_op jit(solution)/shard_map/reduce_scatter | solution.py:51
  365.0 0.0 copy-done.3
  365.0 0.0 copy-done.5
  365.0 0.0 copy-done.6
  365.0 1.7 fusion.45
  366.7 0.0 all-gather.11.cloned.1.call-update
  366.7 0.0 reduce-scatter.9.cloned.1.call-start
  366.8 23.6 %all-gather.11.cloned.1.call-done = f32[1,128,2048]{2,1,0:T(8,128)} async-done(((f32[1,128,256]{2,1,0:T(8,128)}), f32[1,128,2048]{2,1,0:T(8,128)}) %all-gather.11.cloned.1.call-update) | async-done | bytes 1048592 | tf_op jit(solution)/shard_map/all_gather | solution.py:19
  390.4 0.0 copy-start.2
  390.4 7.6 %convolution_bitcast_fusion.2 = f32[1,128,1024]{2,1,0:T(8,128)S(1)} fusion(f32[2048,1024]{1,0:T(8,128)} %all-gather.7.cloned.1.call-done, f32[1,128,2048]{2,1,0:T(8,128)} %all-gather.11.cloned.1.call-done), kind=kOutput, calls=%fused_computation.46 | convolution fusion | flops 3221225472 | bytes 9961472 | tf_op jit(solution)/shard_map/bvc,cn->bvn/dot_general | solution.py:20
  398.0 0.0 slice-start.1
  398.0 1.5 collective-permute-start.3
  399.6 14.4 %collective-permute-done.3 = f32[1,128,1024]{2,1,0:T(8,128)S(1)} collective-permute-done((f32[1,128,1024]{2,1,0:T(8,128)S(1)}, f32[1,128,1024]{2,1,0:T(8,128)S(1)}, u32[]{:S(2)}, u32[]{:S(2)}) %collective-permute-start.3) | collective-permute-done | bytes 524320 | tf_op jit(solution)/shard_map/ppermute | solution.py:29
  414.0 0.0 collective-permute-start.4
  414.0 15.0 %collective-permute-done.4 = f32[1,128,1024]{2,1,0:T(8,128)S(1)} collective-permute-done((f32[1,128,1024]{2,1,0:T(8,128)S(1)}, f32[1,128,1024]{2,1,0:T(8,128)S(1)}, u32[]{:S(2)}, u32[]{:S(2)}) %collective-permute-start.4) | collective-permute-done | bytes 524320 | tf_op jit(solution)/shard_map/ppermute | solution.py:29
  429.0 0.4 collective-permute-start.5
  429.4 14.2 %collective-permute-done.5 = f32[1,128,1024]{2,1,0:T(8,128)S(1)} collective-permute-done((f32[1,128,1024]{2,1,0:T(8,128)S(1)}, f32[1,128,1024]{2,1,0:T(8,128)S(1)}, u32[]{:S(2)}, u32[]{:S(2)}) %collective-permute-start.5) | collective-permute-done | bytes 524320 | tf_op jit(solution)/shard_map/ppermute | solution.py:29
  443.5 0.0 copy-done.2
  443.5 16.8 %fusion.13 = f32[1024,2048]{1,0:T(8,128)S(1)} fusion(f32[512,2048]{1,0:T(8,128)S(1)} %copy-done.2, s32[]{:T(128)S(6)} %select_n.13, f32[1,128,1024]{2,1,0:T(8,128)S(1)} %collective-permute-done.5, f32[1,128,1024]{2,1,0:T(8,128)S(1)} %collective-permute-done.4, f32[1,128,1024]{2,1,0:T(8,128)S(1)} %collective-permute-done.3, ...), kind=kOutput, calls=%fused_computation.31 | convolution fusion | flops 12888571904 | bytes 14680068 | tf_op jit(solution)/shard_map/vm,bvn->bmn/dot_general | solution.py:35
  460.4 0.0 slice-done
  460.4 0.0 slice-done.1
  460.4 15.3 %fusion.33 = f32[1,512,1024]{1,2,0:T(8,128)} fusion(f32[512,2048]{1,0:T(8,128)S(1)} %copy-done.2, f32[1024,2048]{1,0:T(8,128)S(1)} %fusion.13, f32[2048,1024]{0,1:T(8,128)S(1)} %bitcast.84), kind=kOutput, calls=%fused_computation.45 | convolution fusion | flops 12886999040 | bytes 23068672 | tf_op jit(solution)/shard_map/vm,bmn->bvn/dot_general | solution.py:43
  475.7 0.0 reduce-scatter.9.cloned.1.call-update
  475.8 0.0 copy-start.4
  475.8 0.3 reduce-scatter.11.cloned.1.call-start
  476.0 40.7 %reduce-scatter.9.cloned.1.call-done = f32[1,128,1024]{1,2,0:T(8,128)} async-done(((f32[1,512,1024]{1,2,0:T(8,128)}), f32[1,128,1024]{1,2,0:T(8,128)}) %reduce-scatter.9.cloned.1.call-update) | async-done | bytes 524304 | tf_op jit(solution)/shard_map/reduce_scatter | solution.py:50
  516.8 13.4 %convolution_bitcast_fusion = f32[1,128,2048]{2,1,0:T(8,128)} fusion(f32[2048,1024]{1,0:T(8,128)} %all-gather.7.cloned.1.call-done, f32[1,128,1024]{1,2,0:T(8,128)} %reduce-scatter.9.cloned.1.call-done), kind=kOutput, calls=%fused_computation.24 | convolution fusion | flops 3221225472 | bytes 9961472 | tf_op jit(solution)/shard_map/bvn,cn->bvc/dot_general | solution.py:52
  530.2 0.0 reduce-scatter.11.cloned.1.call-update
  530.2 35.3 %reduce-scatter.11.cloned.1.call-done = f32[1,128,256]{2,1,0:T(8,128)} async-done(((f32[1,128,2048]{2,1,0:T(8,128)}), f32[1,128,256]{2,1,0:T(8,128)}) %reduce-scatter.11.cloned.1.call-update) | async-done | bytes 131088 | tf_op jit(solution)/shard_map/reduce_scatter | solution.py:51
  565.5 0.0 copy-done.4
  565.5 1.7 fusion.44
  (2 shorter events, 0.0 us)
Async XLA Ops:
  6.5 28.9 %all-gather.5.cloned.1.call-start = ((), (), s32[]{:S(2)}) async-start(), calls=%async_computation.4 | async-start | bytes 1179648 | tf_op jit(solution)/shard_map/all_gather | solution.py:19
  7.3 179.4 %all-gather.7.cloned.1.call-start = ((), (), s32[]{:S(2)}) async-start(), calls=%async_computation.5 | async-start | bytes 10485760 | tf_op jit(solution)/shard_map/all_gather | solution.py:13
  8.0 225.9 %all-gather.9.cloned.1.call-start = ((), (), s32[]{:S(2)}) async-start(), calls=%async_computation.6 | async-start | bytes 4718592 | tf_op jit(solution)/shard_map/all_gather | solution.py:14
  8.7 307.6 %reduce-scatter.5.cloned.1.call-start = ((), (), s32[]{:S(2)}) async-start(), calls=%async_computation.7 | async-start | bytes 2621440 | tf_op jit(solution)/shard_map/reduce_scatter | solution.py:50
  194.2 15.7 %collective-permute-start = (f32[1,128,1024]{2,1,0:T(8,128)S(1)}, f32[1,128,1024]{2,1,0:T(8,128)S(1)}, u32[]{:S(2)}, u32[]{:S(2)}) collective-permute-start(f32[1,128,1024]{2,1,0:T(8,128)S(1)} %convolution_bitcast_fusion.3), channel_id=1, source_target_pairs={{0,1},{1,2},{2,3},{3,0},{4,5},{5,6},{6,7},{7,4},{8,9},{9,10},{10,1... | collective-permute-start | bytes 1572872 | tf_op jit(solution)/shard_map/ppermute | solution.py:29
  209.8 14.8 %collective-permute-start.1 = (f32[1,128,1024]{2,1,0:T(8,128)S(1)}, f32[1,128,1024]{2,1,0:T(8,128)S(1)}, u32[]{:S(2)}, u32[]{:S(2)}) collective-permute-start(f32[1,128,1024]{2,1,0:T(8,128)S(1)} %collective-permute-done), channel_id=1, source_target_pairs={{0,1},{1,2},{2,3},{3,0},{4,5},{5,6},{6,7},{7,4},{8,9},{9,10},{10,1... | collective-permute-start | bytes 1572872 | tf_op jit(solution)/shard_map/ppermute | solution.py:29
  224.6 14.1 %collective-permute-start.2 = (f32[1,128,1024]{2,1,0:T(8,128)S(1)}, f32[1,128,1024]{2,1,0:T(8,128)S(1)}, u32[]{:S(2)}, u32[]{:S(2)}) collective-permute-start(f32[1,128,1024]{2,1,0:T(8,128)S(1)} %collective-permute-done.1), channel_id=1, source_target_pairs={{0,1},{1,2},{2,3},{3,0},{4,5},{5,6},{6,7},{7,4},{8,9},{9,10},{10,1... | collective-permute-start | bytes 1572872 | tf_op jit(solution)/shard_map/ppermute | solution.py:29
  233.9 24.9 %copy-start.1 = (f32[512,2048]{1,0:T(8,128)S(1)}, f32[512,2048]{1,0:T(8,128)}, u32[]{:S(2)}) copy-start(f32[512,2048]{1,0:T(8,128)} %all-gather.9.cloned.1.call-done) | copy-start | bytes 12582916
  238.7 20.1 %copy-start = (f32[2048,1024]{0,1:T(8,128)S(1)}, f32[2048,1024]{0,1:T(8,128)}, u32[]{:S(2)}) copy-start(f32[2048,1024]{0,1:T(8,128)} %copy.7) | copy-start | bytes 25165828
  274.4 90.7 %copy-start.3 = (f32[1,128,256]{2,1,0:T(8,128)S(1)}, f32[1,128,256]{2,1,0:T(8,128)}, u32[]{:S(2)}) copy-start(f32[1,128,256]{2,1,0:T(8,128)} %param.8) | copy-start | bytes 393220
  274.4 90.6 %copy-start.5 = (f32[256]{0:T(256)S(1)}, f32[256]{0:T(256)}, u32[]{:S(2)}) copy-start(f32[256]{0:T(256)} %param.10) | copy-start | bytes 3076
  274.4 90.6 %copy-start.6 = (f32[128]{0:T(128)S(1)}, f32[128]{0:T(128)}, u32[]{:S(2)}) copy-start(f32[128]{0:T(128)} %param.9) | copy-start | bytes 1540
  274.4 90.6 %reduce-scatter.7.cloned.1.call-start = ((), (), s32[]{:S(2)}) async-start(), calls=%async_computation.8 | async-start | bytes 1179648 | tf_op jit(solution)/shard_map/reduce_scatter | solution.py:51
  329.7 60.7 %all-gather.11.cloned.1.call-start = ((), (), s32[]{:S(2)}) async-start(), calls=%async_computation.9 | async-start | bytes 1179648 | tf_op jit(solution)/shard_map/all_gather | solution.py:19
  366.7 150.0 %reduce-scatter.9.cloned.1.call-start = ((), (), s32[]{:S(2)}) async-start(), calls=%async_computation.10 | async-start | bytes 2621440 | tf_op jit(solution)/shard_map/reduce_scatter | solution.py:50
  390.4 53.2 %copy-start.2 = (f32[512,2048]{1,0:T(8,128)S(1)}, f32[512,2048]{1,0:T(8,128)}, u32[]{:S(2)}) copy-start(f32[512,2048]{1,0:T(8,128)} %all-gather.9.cloned.1.call-done) | copy-start | bytes 12582916
  390.4 70.0 %slice-start = ((s8[8388608]{0:T(1024)(128)(4,1)}), s8[4194304]{0:T(1024)(128)(4,1)S(1)}, s32[]{:S(2)}) async-start(s8[8388608]{0:T(1024)(128)(4,1)} %bitcast.83), calls=%async_computation.12 | async-start | bytes 8388608
  398.0 62.4 %slice-start.1 = ((s8[8388608]{0:T(1024)(128)(4,1)}), s8[4194304]{0:T(1024)(128)(4,1)S(1)}, s32[]{:S(2)}) async-start(s8[8388608]{0:T(1024)(128)(4,1)} %bitcast.83), calls=%async_computation.13 | async-start | bytes 8388608
  398.0 15.9 %collective-permute-start.3 = (f32[1,128,1024]{2,1,0:T(8,128)S(1)}, f32[1,128,1024]{2,1,0:T(8,128)S(1)}, u32[]{:S(2)}, u32[]{:S(2)}) collective-permute-start(f32[1,128,1024]{2,1,0:T(8,128)S(1)} %convolution_bitcast_fusion.2), channel_id=1, source_target_pairs={{0,1},{1,2},{2,3},{3,0},{4,5},{5,6},{6,7},{7,4},{8,9},{9,10},{10,1... | collective-permute-start | bytes 1572872 | tf_op jit(solution)/shard_map/ppermute | solution.py:29
  414.0 15.0 %collective-permute-start.4 = (f32[1,128,1024]{2,1,0:T(8,128)S(1)}, f32[1,128,1024]{2,1,0:T(8,128)S(1)}, u32[]{:S(2)}, u32[]{:S(2)}) collective-permute-start(f32[1,128,1024]{2,1,0:T(8,128)S(1)} %collective-permute-done.3), channel_id=1, source_target_pairs={{0,1},{1,2},{2,3},{3,0},{4,5},{5,6},{6,7},{7,4},{8,9},{9,10},{10,1... | collective-permute-start | bytes 1572872 | tf_op jit(solution)/shard_map/ppermute | solution.py:29
  429.0 14.6 %collective-permute-start.5 = (f32[1,128,1024]{2,1,0:T(8,128)S(1)}, f32[1,128,1024]{2,1,0:T(8,128)S(1)}, u32[]{:S(2)}, u32[]{:S(2)}) collective-permute-start(f32[1,128,1024]{2,1,0:T(8,128)S(1)} %collective-permute-done.4), channel_id=1, source_target_pairs={{0,1},{1,2},{2,3},{3,0},{4,5},{5,6},{6,7},{7,4},{8,9},{9,10},{10,1... | collective-permute-start | bytes 1572872 | tf_op jit(solution)/shard_map/ppermute | solution.py:29
  475.8 89.8 %copy-start.4 = (f32[1,128,256]{2,1,0:T(8,128)S(1)}, f32[1,128,256]{2,1,0:T(8,128)}, u32[]{:S(2)}) copy-start(f32[1,128,256]{2,1,0:T(8,128)} %reduce-scatter.7.cloned.1.call-done) | copy-start | bytes 393220
  475.8 89.8 %reduce-scatter.11.cloned.1.call-start = ((), (), s32[]{:S(2)}) async-start(), calls=%async_computation.11 | async-start | bytes 1179648 | tf_op jit(solution)/shard_map/reduce_scatter | solution.py:51
Sparse Core Ops, SparseCore 0:
  9.2 26.1 all-gather.4
  37.0 149.5 all-gather.6
  188.5 34.7 all-gather.8
  274.5 41.7 reduce-scatter.4
  329.8 35.1 reduce-scatter.6
  366.8 23.4 all-gather.10
  475.9 40.8 reduce-scatter.8
  530.3 35.1 reduce-scatter.10
